TPU v7x, 128 devices: a whole 4x4x4 slice. The times are simulated.
128 devices in a mesh: row: 16 (over y, z_lo, core), col: 8 (over z_hi, x).
Axes of the slice: x: 4, y: 4, z: 4 (z_hi: 2, z_lo: 2; z = z_hi * 2 + z_lo), core: 2. Of those that a mesh axis runs over, the one named last changes fastest.
Arguments:
- samples: bfloat16 [32768, 8192], P(('row', 'col'))
- labels: int32 [32768], P(('row', 'col')), may hold values from 0 to 1
- basis_start: bfloat16 [8192, 256], replicated, may hold values from -0.0625 to 0.0625
- width_index: int32 [], replicated, may hold values from 0 to 2
Outputs:
- projected: bfloat16 [32768, 256], P(('row', 'col'))
- proof: float32 [32768], P(('row', 'col'))
- basis: bfloat16 [8192, 256], replicated
All inputs are finite; a program needn't handle non-finite values.
Results may differ from a plain program's by a relative error of at most 0.011.
Values may be sent and summed in bfloat16 or wider, within the bound.
A program may use at most 128 MiB of HBM per device.

v0:
```python
import math
import jax
import jax.numpy as jnp
from jax import lax
from jax.sharding import PartitionSpec as P


def kernel_sums(panel_rows, panel_cols, col_is_ref, width_sq):
    row_norms = jnp.sum(jnp.square(panel_rows.astype(jnp.float32)), 1)
    col_norms = jnp.sum(jnp.square(panel_cols.astype(jnp.float32)), 1)
    block_size = math.gcd(panel_rows.shape[0], 512)

    def block_sums(pieces):
        block_rows, block_norms = pieces
        inner_products = lax.dot_general(
            block_rows, panel_cols, (((1,), (1,)), ((), ())), preferred_element_type=jnp.float32
        )
        dist_sq = block_norms[:, None] + col_norms[None, :] - 2.0 * inner_products
        kernel = jnp.exp(-dist_sq / (2.0 * width_sq))
        return (jnp.sum(kernel * col_is_ref[None, :], 1), jnp.sum(kernel, 1))

    ref_sums, row_sums = lax.map(
        block_sums,
        (
            panel_rows.reshape(-1, block_size, panel_rows.shape[1]),
            row_norms.reshape(-1, block_size),
        ),
    )
    return (ref_sums.reshape(-1), row_sums.reshape(-1))


def local(samples, labels, basis_start, width_index):
    n_total = jnp.float32(samples.shape[0] * lax.axis_size(("row", "col")))
    is_ref = (labels == 0).astype(jnp.float32)
    column_total, n_ref = lax.psum(
        (jnp.sum(samples, 0, dtype=jnp.float32), jnp.sum(is_ref)), ("row", "col")
    )
    n_cur = n_total - n_ref
    sample_mean = column_total / n_total
    centred = (samples - sample_mean).astype(jnp.bfloat16)
    first = jnp.dot(centred, basis_start, preferred_element_type=jnp.float32).astype(jnp.bfloat16)
    gram_part = (
        lax.dot_general(
            centred, first, (((0,), (0,)), ((), ())), preferred_element_type=jnp.float32
        )
        / n_total
    )
    gram = lax.psum(gram_part, ("row", "col"))
    square = jnp.dot(gram.T, gram, precision=lax.Precision.HIGHEST)
    factor = jnp.linalg.cholesky(square)
    basis = jax.scipy.linalg.solve_triangular(factor, gram.T, lower=True).T.astype(jnp.bfloat16)
    projected = jnp.dot(centred, basis, preferred_element_type=jnp.float32).astype(jnp.bfloat16)
    width_sq = 128.0 * jnp.exp2(width_index.astype(jnp.float32))
    panel_rows = lax.all_gather(projected, "col", axis=0, tiled=True)
    panel_cols, col_is_ref = (
        lax.all_gather(projected, "row", axis=0, tiled=True),
        lax.all_gather(is_ref.astype(jnp.bfloat16), "row", axis=0, tiled=True).astype(is_ref.dtype),
    )
    part_ref, part_rows = kernel_sums(panel_rows, panel_cols, col_is_ref, width_sq)
    ref_sums, row_sums = (
        lax.psum_scatter(part_ref, "col", scatter_dimension=0, tiled=True),
        lax.psum_scatter(part_rows, "col", scatter_dimension=0, tiled=True),
    )
    proof = (ref_sums / n_ref - (row_sums - ref_sums) / n_cur) / (row_sums / n_total)
    return (projected, proof, basis)


def solution(mesh):
    placed = (P(("row", "col"), None), P(("row", "col")), P(), P())
    return jax.shard_map(
        local,
        mesh=mesh,
        in_specs=placed,
        out_specs=(P(("row", "col"), None), P(("row", "col")), P()),
        check_vma=False,
    )
```

profile of v0, /device:TPU:0, one launch (start us, length us, event | category | flops | bytes accessed | tf_op | source)
XLA Modules:
  0.0 501.4 jit_solution(13970861167934475783)
XLA Ops:
  7.2 0.0 all-reduce.7.cloned.1.call-start
  7.2 2.9 convert_reduce_fusion
  10.1 0.6 fusion.26
  10.7 68.6 %all-reduce.3 = (f32[8192]{0:T(1024)S(1)}, f32[]{:T(128)}) all-reduce(f32[8192]{0:T(1024)S(1)} %convert_reduce_fusion, f32[]{:T(128)} %fusion.26), channel_id=1, replica_groups=mesh['row'=16,'col'=8] {'row','col'}, use_global_device_ids=true, to_apply=%region_1.0 | all-reduce | flops 8193 | bytes 65544 | tf_op jit(solution)/shard_map/psum | solution.py:35
  79.3 12.5 %convolution_multiply_fusion = f32[8192,256]{1,0:T(8,128)} fusion(bf16[256,8192]{1,0:T(8,128)(2,1)} %param.6, f32[8192]{0:T(1024)S(1)} %broadcast_multiply_fusion, bf16[8192,256]{1,0:T(8,128)(2,1)} %param.8), kind=kOutput, calls=%fused_computation.8 | convolution fusion | flops 2162229248 | bytes 16809984 | tf_op jit(solution)/shard_map/dot_general | solution.py:43
  91.8 0.3 all-gather.4.cloned.1.call-start
  92.2 157.7 %all-reduce.7.cloned.1.call-done = f32[8192,256]{1,0:T(8,128)} async-done(((f32[8192,256]{1,0:T(8,128)}), f32[8192,256]{1,0:T(8,128)}) %all-reduce.7.cloned.1.call-update) | async-done | bytes 8388624 | tf_op jit(solution)/shard_map/psum | solution.py:48
  249.9 19.5 %fusion.32 = f32[256,256]{1,0:T(8,128)S(1)} fusion(f32[8192,256]{1,0:T(8,128)} %all-reduce.7.cloned.1.call-done), kind=kOutput, calls=%fused_computation.55 | convolution fusion | flops 6442450944 | bytes 8650752 | tf_op jit(solution)/shard_map/dot_general | solution.py:49
  269.5 0.1 copy.9
  269.7 11.7 %cholesky.50 = f32[128,128]{1,0:T(8,128)S(1)} custom-call(f32[128,128]{1,0:T(8,128)S(1)} %cholesky.118), custom_call_target="Cholesky" | custom-call | tf_op jit(solution)/shard_map/jit(cholesky)/cholesky | solution.py:50
  281.4 9.8 %custom-call.15 = f32[1,128,128]{1,2,0:T(8,128)S(1)} custom-call(f32[1,128,128]{2,1,0:T(8,128)S(1)} %get-tuple-element.162), custom_call_target="InvertDiagBlocksLowerTriangular" | custom-call | tf_op jit(solution)/shard_map/jit(cholesky)/cholesky | solution.py:50
  291.3 0.2 constant_dynamic-update-slice_fusion.1
  291.5 0.3 convolution_subtract_fusion.1
  291.8 11.7 %cholesky.105 = f32[128,128]{1,0:T(8,128)S(1)} custom-call(f32[128,128]{1,0:T(8,128)S(1)} %convolution_subtract_fusion.1), custom_call_target="Cholesky" | custom-call | tf_op jit(solution)/shard_map/jit(cholesky)/cholesky | solution.py:50
  303.5 0.6 compare_reduce_fusion
  305.5 0.1 triangular_solve.59
  305.6 4.0 while.16
  305.6 0.6 fusion.46
  306.1 1.4 bitcast_dynamic-update-slice_fusion.2
  307.6 0.6 fusion.46
  308.2 1.4 bitcast_dynamic-update-slice_fusion.2
  309.5 19.8 %custom-call.16 = f32[2,128,128]{1,2,0:T(8,128)S(1)} custom-call(f32[2,128,128]{2,1,0:T(8,128)S(1)} %get-tuple-element.118), custom_call_target="InvertDiagBlocksLowerTriangular" | custom-call | tf_op jit(solution)/shard_map/jit(_solve_triangular)/triangular_solve | solution.py:51
  329.4 5.7 %fusion.31 = (bf16[128,8192]{1,0:T(8,128)(2,1)S(1)}, f32[128,8192]{1,0:T(8,128)S(1)}) fusion(f32[256,8192]{0,1:T(8,128)} %bitcast.65, f32[2,128,128]{1,2,0:T(8,128)S(1)} %custom-call.16), kind=kOutput, calls=%fused_computation.54 | convolution fusion | flops 1611661312 | bytes 10551296 | tf_op jit(solution)/shard_map/jit(_solve_triangular)/triangular_solve | solution.py:51
  335.1 6.7 %convolution_subtract_fusion = f32[128,8192]{0,1:T(8,128)S(1)} fusion(f32[128,8192]{1,0:T(8,128)S(1)} %get-tuple-element.166, f32[256,8192]{0,1:T(8,128)S(1)} %bitcast.66, f32[256,256]{1,0:T(8,128)S(1)} %get-tuple-element.312), kind=kOutput, calls=%fused_computation.11 | convolution fusion | flops 1611661312 | bytes 12648448 | tf_op jit(solution)/shard_map/jit(_solve_triangular)/triangular_solve | solution.py:51
  341.8 4.1 convolution_convert_fusion
  345.9 1.3 copy-done.2
  347.3 2.1 fusion.15
  349.4 0.0 all-gather.6.cloned.1.call-start
  349.5 0.7 all-gather.6.cloned.1.call-update
  350.2 17.6 %all-gather = bf16[16,1,256]{2,1,0:T(2,128)(2,1)S(1)} all-gather(bf16[1,1,256]{2,1,0:T(2,128)(2,1)S(1)} %reshape.65), channel_id=1, replica_groups=mesh['row'=16,'col'=8] {'row'}, dimensions={0}, use_global_device_ids=true | all-gather | bytes 8704 | tf_op jit(solution)/shard_map/all_gather | solution.py:57
  369.1 0.7 dynamic-slice.3
  370.4 3.9 fusion.11
  374.3 6.4 %copy.10 = bf16[8192,256]{1,0:T(8,128)(2,1)} copy(bf16[8192,256]{0,1:T(8,128)(2,1)} %fusion.11) | data formatting | bytes 8388608
  380.7 14.3 %all-gather.4.cloned.1.call-done = bf16[2048,256]{1,0:T(8,128)(2,1)} async-done(((bf16[256,256]{1,0:T(8,128)(2,1)}), bf16[2048,256]{1,0:T(8,128)(2,1)}) %all-gather.4.cloned.1.call-update) | async-done | bytes 1048592 | tf_op jit(solution)/shard_map/all_gather | solution.py:54
  394.9 1.6 multiply_reduce_fusion.2
  396.5 33.2 %all-gather.6.cloned.1.call-done = bf16[4096,256]{1,0:T(8,128)(2,1)} async-done(((bf16[256,256]{1,0:T(8,128)(2,1)}), bf16[4096,256]{1,0:T(8,128)(2,1)}) %all-gather.6.cloned.1.call-update) | async-done | bytes 2097168 | tf_op jit(solution)/shard_map/all_gather | solution.py:56
  429.7 2.2 multiply_reduce_fusion.1
  431.9 19.9 %while.15 = (s32[]{:T(128)}, f32[4,512]{1,0:T(4,128)S(1)}, f32[4,512]{1,0:T(4,128)S(1)}, f32[4,512]{1,0:T(4,128)S(1)}, f32[4096]{0:T(1024)S(1)}, /*index=5*/bf16...) while((s32[]{:T(128)}, f32[4,512]{1,0:T(4,128)S(1)}, ...), condition=%wide.region_12.13_spmd, body=%wide.region_9.12_spmd.sunk | while | flops 1090518016 | bytes 2411641 | solution.py:22
  432.0 4.8 fusion.45
  436.9 0.1 dynamic_update_slice.14
  436.9 4.8 fusion.45
  441.8 0.1 dynamic_update_slice.14
  441.9 4.8 fusion.45
  446.8 0.1 dynamic_update_slice.14
  446.9 4.8 fusion.45
  451.8 0.1 dynamic_update_slice.14
  451.9 41.5 %all-reduce.4 = (f32[2048]{0:T(1024)S(1)}, f32[2048]{0:T(1024)S(1)}) all-reduce(f32[2048]{0:T(1024)S(1)} %bitcast.72, f32[2048]{0:T(1024)S(1)} %bitcast.71), channel_id=3, replica_groups=mesh['row'=16,'col'=8] {'col'}, use_global_device_ids=true, to_apply=%region_16.17.clone | all-reduce | flops 4096 | bytes 32768
  493.4 1.2 fusion.25
  (38 shorter events, 0.5 us)
Async XLA Ops:
  7.2 2.9 copy-start.3
  7.2 242.8 %all-reduce.7.cloned.1.call-start = ((), (), s32[]{:S(2)}) async-start(), calls=%async_computation | async-start | bytes 16777216 | tf_op jit(solution)/shard_map/psum | solution.py:48
  91.8 303.1 %all-gather.4.cloned.1.call-start = ((), (), s32[]{:S(2)}) async-start(), calls=%async_computation.1 | async-start | bytes 1179648 | tf_op jit(solution)/shard_map/all_gather | solution.py:54
  329.4 5.7 %copy-start = (f32[8192,256]{1,0:T(8,128)S(1)}, f32[8192,256]{1,0:T(8,128)}, u32[]{:S(2)}) copy-start(f32[8192,256]{1,0:T(8,128)} %all-reduce.7.cloned.1.call-done) | copy-start | bytes 25165828
  341.8 5.5 %copy-start.1 = (bf16[256,8192]{1,0:T(8,128)(2,1)S(1)}, bf16[256,8192]{1,0:T(8,128)(2,1)}, u32[]{:S(2)}) copy-start(bf16[256,8192]{1,0:T(8,128)(2,1)} %param.6) | copy-start | bytes 12582916
  345.9 1.3 copy-start.2
  347.3 21.8 %copy-start.4 = (u32[128]{0:T(128)S(1)}, u32[128]{0:T(128)}, u32[]{:S(2)}) copy-start(u32[128]{0:T(128)} %constant.145) | copy-start | bytes 1540
  349.4 80.3 %all-gather.6.cloned.1.call-start = ((), (), s32[]{:S(2)}) async-start(), calls=%async_computation.2 | async-start | bytes 2228224 | tf_op jit(solution)/shard_map/all_gather | solution.py:56
Sparse Core Ops, SparseCore 0:
  91.9 157.9 all-reduce.6
  349.5 45.3 all-gather.3
  397.2 32.4 all-gather.5
where the time goes:
time: 507 us; the launch traced here: 501 us
  waiting for transfers between devices  206 us (41%)
  blocking collectives  128 us (25%)
  matrix products  70.5 us (14%)
  other arithmetic  66.2 us (13%)
  between operations  17.5 us (3%)
  local copies, waits for them, and re-layouts  13 us (3%)
    psum x1, waiting for transfers between devices, local(): gram = lax.psum(gram_part, ('row', 'col'))  158 us
    psum x1, blocking collectives, local(): lax.psum((jnp.sum(samples, 0, dtype=jnp.float32), jnp.sum(is_ref)), ('row...  68.6 us
    unnamed x1, blocking collectives  41.5 us
    another operation x6, other arithmetic, local(): factor = jnp.linalg.cholesky(square)  34 us
    all_gather x1, waiting for transfers between devices, local(): lax.all_gather(projected, 'row', axis=0, tiled=True)  33.2 us
    another operation x3, other arithmetic, local(): jax.scipy.linalg.solve_triangular(factor, gram.T, lower=True)  19.9 us
    dot_general x1, matrix products, local(): square = jnp.dot(gram.T, gram, precision=lax.Precision.HIGHEST)  19.5 us
    dot_general x4, matrix products, block_sums(): lax.dot_general(block_rows, panel_cols, (((1,), (1,)), ((), ())), preferr...  19.4 us
  transfers between devices with their start and end apart: 3, of which 3 were waited for; matrix products, arithmetic and copies ran while one was open for 2% of the time, Pallas kernels for 0%

commit v1 on v0

--- a/solution.py
+++ b/solution.py
@@ -3,6 +3,11 @@
 import jax.numpy as jnp
 from jax import lax
 from jax.sharding import PartitionSpec as P
+
+
+def axis_by_axis(x, leading, second):
+    partial = lax.psum(x, leading)
+    return lax.psum(partial, second)
 
 
 def kernel_sums(panel_rows, panel_cols, col_is_ref, width_sq):
@@ -45,7 +50,7 @@
         )
         / n_total
     )
-    gram = lax.psum(gram_part, ("row", "col"))
+    gram = axis_by_axis(gram_part, "col", "row")
     square = jnp.dot(gram.T, gram, precision=lax.Precision.HIGHEST)
     factor = jnp.linalg.cholesky(square)
     basis = jax.scipy.linalg.solve_triangular(factor, gram.T, lower=True).T.astype(jnp.bfloat16)

time: 507 us -> 729 us (1.44)
  waiting for transfers between devices: 206 us -> 425 us
    psum x1 -> x2, waiting for transfers between devices: 158 us -> 375 us  [the longest x1 193 us: axis_by_axis(): return lax.psum(partial, second)]
  transfers between devices with their start and end apart: 3 -> 4, of which waited for: 3 -> 4; matrix products, arithmetic and copies ran while one was open for 2% -> 2% of each run, Pallas kernels for 0% -> 0%
where the time goes in v1:
time: 729 us; the launch traced here: 723 us
  waiting for transfers between devices  425 us (58%)
  blocking collectives  130 us (18%)
  matrix products  70.8 us (10%)
  other arithmetic  66.3 us (9%)
  between operations  17.5 us (2%)
  local copies, waits for them, and re-layouts  13 us (2%)
    psum x1, waiting for transfers between devices, axis_by_axis(): return lax.psum(partial, second)  193 us
    psum x1, waiting for transfers between devices, axis_by_axis(): partial = lax.psum(x, leading)  182 us
    psum x1, blocking collectives, local(): lax.psum((jnp.sum(samples, 0, dtype=jnp.float32), jnp.sum(is_ref)), ('row...  68.6 us
    unnamed x1, blocking collectives  41.6 us
    another operation x6, other arithmetic, local(): factor = jnp.linalg.cholesky(square)  34 us
    all_gather x1, waiting for transfers between devices, local(): lax.all_gather(projected, 'row', axis=0, tiled=True)  33 us
    another operation x3, other arithmetic, local(): jax.scipy.linalg.solve_triangular(factor, gram.T, lower=True)  19.9 us
    all_gather x1, blocking collectives, local(): lax.all_gather(is_ref.astype(jnp.bfloat16), 'row', axis=0, tiled=True)  19.9 us
  transfers between devices with their start and end apart: 4, of which 4 were waited for; matrix products, arithmetic and copies ran while one was open for 2% of the time, Pallas kernels for 0%

profile of v1, /device:TPU:0, one launch (start us, length us, event | category | flops | bytes accessed | tf_op | source)
XLA Modules:
  0.0 723.4 jit_solution(13633976410314339938)
XLA Ops:
  7.2 2.9 convert_reduce_fusion
  10.1 0.6 fusion.26
  10.7 68.6 %all-reduce.3 = (f32[8192]{0:T(1024)S(1)}, f32[]{:T(128)}) all-reduce(f32[8192]{0:T(1024)S(1)} %convert_reduce_fusion, f32[]{:T(128)} %fusion.26), channel_id=1, replica_groups=mesh['row'=16,'col'=8] {'row','col'}, use_global_device_ids=true, to_apply=%region_1.0 | all-reduce | flops 8193 | bytes 65544 | tf_op jit(solution)/shard_map/psum | solution.py:40
  79.3 12.5 %convolution_multiply_fusion = f32[8192,256]{1,0:T(8,128)} fusion(bf16[256,8192]{1,0:T(8,128)(2,1)} %param.6, f32[8192]{0:T(1024)S(1)} %broadcast_multiply_fusion, bf16[8192,256]{1,0:T(8,128)(2,1)} %param.8), kind=kOutput, calls=%fused_computation.8 | convolution fusion | flops 2162229248 | bytes 16809984 | tf_op jit(solution)/shard_map/dot_general | solution.py:48
  91.9 182.2 %all-reduce.8.cloned.1.call-done = f32[8192,256]{1,0:T(8,128)} async-done(((f32[8192,256]{1,0:T(8,128)}), f32[8192,256]{1,0:T(8,128)}) %all-reduce.8.cloned.1.call-update) | async-done | bytes 8388624 | tf_op jit(solution)/shard_map/psum | solution.py:9
  274.1 0.3 all-gather.4.cloned.1.call-start
  274.5 193.1 %all-reduce.10.cloned.1.call-done = f32[8192,256]{1,0:T(8,128)} async-done(((f32[8192,256]{1,0:T(8,128)}), f32[8192,256]{1,0:T(8,128)}) %all-reduce.10.cloned.1.call-update) | async-done | bytes 8388624 | tf_op jit(solution)/shard_map/psum | solution.py:10
  467.6 19.8 %fusion.32 = f32[256,256]{1,0:T(8,128)S(1)} fusion(f32[8192,256]{1,0:T(8,128)} %all-reduce.10.cloned.1.call-done), kind=kOutput, calls=%fused_computation.55 | convolution fusion | flops 6442450944 | bytes 8650752 | tf_op jit(solution)/shard_map/dot_general | solution.py:54
  487.4 0.1 copy.9
  487.6 11.7 %cholesky.50 = f32[128,128]{1,0:T(8,128)S(1)} custom-call(f32[128,128]{1,0:T(8,128)S(1)} %cholesky.118), custom_call_target="Cholesky" | custom-call | tf_op jit(solution)/shard_map/jit(cholesky)/cholesky | solution.py:55
  499.3 9.8 %custom-call.15 = f32[1,128,128]{1,2,0:T(8,128)S(1)} custom-call(f32[1,128,128]{2,1,0:T(8,128)S(1)} %get-tuple-element.162), custom_call_target="InvertDiagBlocksLowerTriangular" | custom-call | tf_op jit(solution)/shard_map/jit(cholesky)/cholesky | solution.py:55
  509.2 0.2 constant_dynamic-update-slice_fusion.1
  509.4 0.3 convolution_subtract_fusion.1
  509.7 11.7 %cholesky.105 = f32[128,128]{1,0:T(8,128)S(1)} custom-call(f32[128,128]{1,0:T(8,128)S(1)} %convolution_subtract_fusion.1), custom_call_target="Cholesky" | custom-call | tf_op jit(solution)/shard_map/jit(cholesky)/cholesky | solution.py:55
  521.4 0.6 compare_reduce_fusion
  523.4 0.1 triangular_solve.59
  523.5 4.0 while.16
  523.5 0.6 fusion.46
  524.1 1.4 bitcast_dynamic-update-slice_fusion.2
  525.5 0.6 fusion.46
  526.1 1.4 bitcast_dynamic-update-slice_fusion.2
  527.5 19.8 %custom-call.16 = f32[2,128,128]{1,2,0:T(8,128)S(1)} custom-call(f32[2,128,128]{2,1,0:T(8,128)S(1)} %get-tuple-element.118), custom_call_target="InvertDiagBlocksLowerTriangular" | custom-call | tf_op jit(solution)/shard_map/jit(_solve_triangular)/triangular_solve | solution.py:56
  547.3 5.7 fusion.31
  553.0 6.7 convolution_subtract_fusion
  559.7 4.1 convolution_convert_fusion
  563.9 1.3 copy-done.2
  565.2 2.1 fusion.15
  567.3 0.0 all-gather.6.cloned.1.call-start
  567.4 0.5 all-gather.6.cloned.1.call-update
  568.0 19.9 %all-gather = bf16[16,1,256]{2,1,0:T(2,128)(2,1)S(1)} all-gather(bf16[1,1,256]{2,1,0:T(2,128)(2,1)S(1)} %reshape.65), channel_id=1, replica_groups=mesh['row'=16,'col'=8] {'row'}, dimensions={0}, use_global_device_ids=true | all-gather | bytes 8704 | tf_op jit(solution)/shard_map/all_gather | solution.py:62
  589.1 0.7 dynamic-slice.3
  590.5 3.9 fusion.11
  594.4 6.4 copy.10
  600.7 16.3 %all-gather.4.cloned.1.call-done = bf16[2048,256]{1,0:T(8,128)(2,1)} async-done(((bf16[256,256]{1,0:T(8,128)(2,1)}), bf16[2048,256]{1,0:T(8,128)(2,1)}) %all-gather.4.cloned.1.call-update) | async-done | bytes 1048592 | tf_op jit(solution)/shard_map/all_gather | solution.py:59
  617.0 1.6 multiply_reduce_fusion.2
  618.6 33.0 %all-gather.6.cloned.1.call-done = bf16[4096,256]{1,0:T(8,128)(2,1)} async-done(((bf16[256,256]{1,0:T(8,128)(2,1)}), bf16[4096,256]{1,0:T(8,128)(2,1)}) %all-gather.6.cloned.1.call-update) | async-done | bytes 2097168 | tf_op jit(solution)/shard_map/all_gather | solution.py:61
  651.7 2.2 multiply_reduce_fusion.1
  653.9 19.9 %while.15 = (s32[]{:T(128)}, f32[4,512]{1,0:T(4,128)S(1)}, f32[4,512]{1,0:T(4,128)S(1)}, f32[4,512]{1,0:T(4,128)S(1)}, f32[4096]{0:T(1024)S(1)}, /*index=5*/bf16...) while((s32[]{:T(128)}, f32[4,512]{1,0:T(4,128)S(1)}, ...), condition=%wide.region_13.14_spmd, body=%wide.region_10.13_spmd.sunk | while | flops 1090518016 | bytes 2411641 | solution.py:27
  653.9 4.8 fusion.45
  658.8 0.1 dynamic_update_slice.14
  658.9 4.8 fusion.45
  663.8 0.1 dynamic_update_slice.14
  663.8 4.8 fusion.45
  668.7 0.1 dynamic_update_slice.14
  668.8 4.8 fusion.45
  673.7 0.1 dynamic_update_slice.14
  673.8 41.6 %all-reduce.4 = (f32[2048]{0:T(1024)S(1)}, f32[2048]{0:T(1024)S(1)}) all-reduce(f32[2048]{0:T(1024)S(1)} %bitcast.72, f32[2048]{0:T(1024)S(1)} %bitcast.71), channel_id=3, replica_groups=mesh['row'=16,'col'=8] {'col'}, use_global_device_ids=true, to_apply=%region_17.18.clone | all-reduce | flops 4096 | bytes 32768
  715.4 1.2 fusion.25
  (41 shorter events, 0.6 us)
Async XLA Ops:
  7.2 2.9 copy-start.3
  7.2 266.9 %all-reduce.8.cloned.1.call-start = ((), (), s32[]{:S(2)}) async-start(), calls=%async_computation | async-start | bytes 16777216 | tf_op jit(solution)/shard_map/psum | solution.py:9
  91.8 375.7 %all-reduce.10.cloned.1.call-start = ((), (), s32[]{:S(2)}) async-start(), calls=%async_computation.1 | async-start | bytes 16777216 | tf_op jit(solution)/shard_map/psum | solution.py:10
  274.1 342.9 %all-gather.4.cloned.1.call-start = ((), (), s32[]{:S(2)}) async-start(), calls=%async_computation.2 | async-start | bytes 1179648 | tf_op jit(solution)/shard_map/all_gather | solution.py:59
  547.3 5.7 copy-start
  559.7 5.5 copy-start.1
  563.9 1.3 copy-start.2
  565.2 23.9 %copy-start.4 = (u32[128]{0:T(128)S(1)}, u32[128]{0:T(128)}, u32[]{:S(2)}) copy-start(u32[128]{0:T(128)} %constant.145) | copy-start | bytes 1540
  567.3 84.3 %all-gather.6.cloned.1.call-start = ((), (), s32[]{:S(2)}) async-start(), calls=%async_computation.3 | async-start | bytes 2228224 | tf_op jit(solution)/shard_map/all_gather | solution.py:61
Sparse Core Ops, SparseCore 0:
  91.9 182.1 all-reduce.7
  276.6 190.8 all-reduce.9
  567.4 49.5 all-gather.3
  619.1 32.4 all-gather.5
